TPU v7x, 128 devices: a whole 4x4x4 slice. The times are simulated.
128 devices in a mesh: section: 8 (over z, x_lo), dp: 16 (over y, x_hi, core).
Axes of the slice: x: 4 (x_hi: 2, x_lo: 2; x = x_hi * 2 + x_lo), y: 4, z: 4, core: 2. Of those that a mesh axis runs over, the one named last changes fastest.
Arguments:
- master: float32 [8, 2560, 2560], P('section', 'dp'), may hold values from -0.125 to 0.125
- first_moment: float32 [8, 2560, 2560], P('section', 'dp'), may hold values from -3 to 3
- second_moment: float32 [8, 2560, 2560], P('section', 'dp'), may hold values from 0.1 to 4
- inputs_own: bfloat16 [8, 4, 2048, 2560], P('section', None, 'dp'), may hold values from -6 to 6
- inputs_arriving: bfloat16 [8, 4, 2048, 2560], P('section', None, 'dp'), may hold values from -6 to 6
- grads_own: bfloat16 [8, 4, 2048, 2560], P('section', None, 'dp'), may hold values from -0.13183594 to 0.13183594
- windows_own: int32 [8, 2048, 2560], P('section', 'dp'), may hold values from 0 to 15
- windows_arriving: int32 [8, 2048, 2560], P('section', 'dp'), may hold values from 0 to 15
- next_inputs: bfloat16 [8, 512, 2560], P('section', 'dp'), may hold values from -6 to 6
Outputs:
- fresh_params: float32 [8, 2560, 2560], P('section', 'dp')
- fresh_first: float32 [8, 2560, 2560], P('section', 'dp')
- fresh_second: float32 [8, 2560, 2560], P('section', 'dp')
- next_currents: bfloat16 [8, 512, 2560], P('section', 'dp')
Inputs may be any that keep to these rules, and one draw needn't show every extreme that they name: `windows_own`: bit t of an entry is the surrogate derivative of spikes_t by v_t for timestep t. `windows_arriving`: bit t of an entry is the surrogate derivative of spikes_t by v_t for timestep t.
All inputs are finite; a program needn't handle non-finite values.
Results may differ from a plain program's by a relative error of at most 0.008.
Values may be sent and summed in bfloat16 or wider, within the bound.
A program may use at most 128 MiB of HBM per device.

v0:
```python
import jax
import jax.numpy as jnp
from jax import lax
from jax.sharding import PartitionSpec as P

LEAK_RATE = 0.5
LEARN_RATE = 0.002
FIRST_DECAY = 0.9
SECOND_DECAY = 0.95
EPSILON = 1e-08
WEIGHT_DECAY = 0.1
FIRST_CORRECTION = 1.0 - 0.9**10
SECOND_CORRECTION = 1.0 - 0.95**10


def passed_along(shard, axis, by):
    count = lax.axis_size(axis)
    pairs = [(i, i + by) for i in range(count) if 0 <= i + by < count]
    return lax.ppermute(shard, axis, pairs)


def membrane_grads(gradients, windows):
    carried = jnp.zeros(gradients.shape[1:], jnp.float32)
    results = []
    for moment in reversed(range(gradients.shape[0])):
        window = jnp.bitwise_and(jnp.right_shift(windows, moment), 1).astype(jnp.float32)
        carried = window * gradients[moment].astype(jnp.float32) + LEAK_RATE * carried
        results = [carried] + results
    return jnp.stack(results).astype(jnp.bfloat16)


def shards(
    master,
    first_moment,
    second_moment,
    inputs_own,
    inputs_arriving,
    grads_own,
    windows_own,
    windows_arriving,
    next_inputs,
):
    params = master[0]
    timesteps, tok_rows, features = (grads_own.shape[1], grads_own.shape[2], grads_own.shape[3])
    flat_rows = timesteps * tok_rows
    membrane_own = membrane_grads(grads_own[0], windows_own[0]).reshape(flat_rows, features)
    through = lax.dot_general(
        membrane_own,
        lax.all_gather(params.astype(jnp.bfloat16), "dp", axis=0, tiled=True),
        (((1,), (1,)), ((), ())),
        preferred_element_type=jnp.float32,
    )
    outgoing = (grads_own[0].reshape(flat_rows, features).astype(jnp.float32) + through).astype(
        jnp.bfloat16
    )
    received = passed_along(outgoing.reshape(timesteps, tok_rows, features), "section", -1)
    membrane_arriving = membrane_grads(received, windows_arriving[0]).reshape(flat_rows, features)
    acts_own = inputs_own[0].reshape(flat_rows, features)
    acts_arriving = inputs_arriving[0].reshape(flat_rows, features)
    contract = (((0,), (0,)), ((), ()))
    partial_value = lax.dot_general(
        acts_own, membrane_own, contract, preferred_element_type=jnp.float32
    )
    gradient = lax.psum_scatter(
        (
            partial_value
            + lax.dot_general(
                acts_arriving, membrane_arriving, contract, preferred_element_type=jnp.float32
            )
        ).astype(jnp.bfloat16),
        "dp",
        scatter_dimension=0,
        tiled=True,
    ).astype(jnp.float32)
    fresh_first = FIRST_DECAY * first_moment[0] + (1.0 - FIRST_DECAY) * gradient
    fresh_second = SECOND_DECAY * second_moment[0] + (1.0 - SECOND_DECAY) * gradient * gradient
    direction = (
        fresh_first / FIRST_CORRECTION / (jnp.sqrt(fresh_second / SECOND_CORRECTION) + EPSILON)
    )
    fresh_params = params - LEARN_RATE * (direction + WEIGHT_DECAY * params)
    fresh_weights = fresh_params.astype(jnp.bfloat16)
    upcoming = next_inputs[0]
    currents = jnp.dot(
        upcoming,
        lax.all_gather(fresh_weights, "dp", axis=0, tiled=True),
        preferred_element_type=jnp.float32,
    )
    next_currents = currents.astype(jnp.bfloat16)
    return (fresh_params[None], fresh_first[None], fresh_second[None], next_currents[None])


def solution(mesh):
    return jax.shard_map(
        shards,
        mesh=mesh,
        in_specs=(
            P("section", "dp", None),
            P("section", "dp", None),
            P("section", "dp", None),
            P("section", None, "dp", None),
            P("section", None, "dp", None),
            P("section", None, "dp", None),
            P("section", "dp", None),
            P("section", "dp", None),
            P("section", "dp", None),
        ),
        out_specs=(
            P("section", "dp", None),
            P("section", "dp", None),
            P("section", "dp", None),
            P("section", "dp", None),
        ),
        check_vma=False,
    )
```

profile of v0, /device:TPU:1, one launch (start us, length us, event | category | flops | bytes accessed | tf_op | source)
XLA Modules:
  0.0 454.4 jit_solution(939705589628608496)
XLA Ops:
  7.2 0.0 copy-start
  7.2 0.0 all-gather.3.cloned.1.call-start
  7.2 2.6 bitcast_convert_fusion
  9.8 0.0 all-gather.3.cloned.1.call-update
  9.8 0.0 reduce-scatter.4.cloned.1.call-start
  9.9 3.2 fusion.9
  13.1 1.8 maximum_convert_fusion
  14.9 92.3 %all-gather.3.cloned.1.call-done = bf16[2560,2560]{1,0:T(8,128)(2,1)} async-done(((bf16[160,2560]{1,0:T(8,128)(2,1)}), bf16[2560,2560]{1,0:T(8,128)(2,1)}) %all-gather.3.cloned.1.call-update) | async-done | bytes 13107216 | tf_op jit(solution)/shard_map/all_gather | solution.py:49
  107.2 0.0 copy-start.3
  107.2 13.9 %fusion.1 = bf16[512,2560]{1,0:T(8,128)(2,1)} fusion(bf16[512,2560]{1,0:T(8,128)(2,1)} %bitcast.79, bf16[512,2560]{1,0:T(8,128)(2,1)} %bitcast.80, bf16[2560,2560]{1,0:T(8,128)(2,1)} %all-gather.3.cloned.1.call-done), kind=kOutput, calls=%fused_computation.4 | convolution fusion | flops 6714818560 | bytes 20971520 | tf_op jit(solution)/shard_map/dot_general | solution.py:47
  121.1 1.5 collective-permute-start
  122.6 0.0 copy-done
  122.6 0.0 copy-done.3
  122.6 0.0 copy-start.4
  122.6 12.3 %fusion.17 = f32[2560,2560]{1,0:T(8,128)} fusion(bf16[512,2560]{1,0:T(8,128)(2,1)S(1)} %bitcast.81, bf16[512,2560]{1,0:T(8,128)(2,1)S(1)} %bitcast.78), kind=kOutput, calls=%fused_computation.35 | convolution fusion | flops 6710886400 | bytes 31457280 | tf_op jit(solution)/shard_map/dot_general | solution.py:61
  134.9 46.4 %collective-permute-done = bf16[4,128,2560]{2,1,0:T(8,128)(2,1)S(1)} collective-permute-done((bf16[4,128,2560]{2,1,0:T(8,128)(2,1)}, bf16[4,128,2560]{2,1,0:T(8,128)(2,1)S(1)}, u32[]{:S(2)}, u32[]{:S(2)}) %collective-permute-start) | collective-permute-done | bytes 2621472 | tf_op jit(solution)/shard_map/ppermute | solution.py:19
  181.4 0.0 copy-done.4
  181.4 1.2 add_convert_fusion.1
  182.5 1.8 pad_maximum_fusion
  184.4 16.4 %fusion = bf16[2560,2560]{0,1:T(8,128)(2,1)} fusion(f32[2560,2560]{1,0:T(8,128)} %fusion.17, bf16[512,2560]{1,0:T(8,128)(2,1)} %bitcast.82, bf16[512,2560]{1,0:T(8,128)(2,1)} %bitcast.84), kind=kOutput, calls=%fused_computation.1 | convolution fusion | flops 6723993600 | bytes 44564480 | tf_op jit(solution)/shard_map/dot_general | solution.py:67
  200.8 17.7 %copy.20 = bf16[2560,2560]{1,0:T(8,128)(2,1)} copy(bf16[2560,2560]{0,1:T(8,128)(2,1)} %fusion) | data formatting | bytes 26214400
  218.4 0.0 copy-start.2
  218.4 0.0 reduce-scatter.4.cloned.1.call-update
  218.5 0.0 copy-start.5
  218.5 0.0 all-gather.5.cloned.1.call-start
  218.5 123.0 %reduce-scatter.4.cloned.1.call-done = bf16[160,2560]{1,0:T(8,128)(2,1)} async-done(((bf16[2560,2560]{1,0:T(8,128)(2,1)}), bf16[160,2560]{1,0:T(8,128)(2,1)}) %reduce-scatter.4.cloned.1.call-update) | async-done | bytes 819216 | tf_op jit(solution)/shard_map/reduce_scatter | solution.py:64
  341.5 0.0 copy-done.2
  341.5 6.0 %fusion.16 = (bf16[160,2560]{1,0:T(8,128)(2,1)}, f32[160,2560]{1,0:T(8,128)}, f32[1,160,2560]{2,1,0:T(8,128)}, f32[1,160,2560]{2,1,0:T(8,128)}) fusion(f32[1,160,2560]{2,1,0:T(8,128)} %param.11, bf16[160,2560]{1,0:T(8,128)(2,1)} %reduce-scatter.4.cloned.1.call-done, f32[1,160,2560]{2,1,0:T(8,128)} %param.10, f32[1,160,2560]{2,1,0:T(8,128)S(1)} %copy-done.2), kind=kLoop, calls=%fused_computation.34 | loop fusion | flops 6963200 | bytes 11468800 | tf_op jit(solution)/shard_map/convert_element_type | solution.py:81
  347.5 0.0 all-gather.5.cloned.1.call-update
  347.5 92.4 %all-gather.5.cloned.1.call-done = bf16[2560,2560]{1,0:T(8,128)(2,1)} async-done(((bf16[160,2560]{1,0:T(8,128)(2,1)}), bf16[2560,2560]{1,0:T(8,128)(2,1)}) %all-gather.5.cloned.1.call-update) | async-done | bytes 13107216 | tf_op jit(solution)/shard_map/all_gather | solution.py:85
  439.9 0.0 copy-done.5
  439.9 0.0 copy-start.1
  439.9 7.9 %fusion.2 = bf16[1,32,2560]{2,1,0:T(8,128)(2,1)} fusion(bf16[2560,2560]{1,0:T(8,128)(2,1)} %all-gather.5.cloned.1.call-done, bf16[1,32,2560]{2,1,0:T(8,128)(2,1)S(1)} %copy-done.5), kind=kOutput, calls=%fused_computation.6 | convolution fusion | flops 419512320 | bytes 13434880 | tf_op jit(solution)/shard_map/dot_general | solution.py:83
  447.8 0.0 copy-done.1
Async XLA Ops:
  7.2 115.4 %copy-start = (bf16[1,4,128,2560]{3,2,1,0:T(8,128)(2,1)S(1)}, bf16[1,4,128,2560]{3,2,1,0:T(8,128)(2,1)}, u32[]{:S(2)}) copy-start(bf16[1,4,128,2560]{3,2,1,0:T(8,128)(2,1)} %param.12) | copy-start | bytes 7864324
  7.2 100.0 %all-gather.3.cloned.1.call-start = ((), (), s32[]{:S(2)}) async-start(), calls=%async_computation.1 | async-start | bytes 13926400 | tf_op jit(solution)/shard_map/all_gather | solution.py:49
  9.8 331.7 %reduce-scatter.4.cloned.1.call-start = ((), (), s32[]{:S(2)}) async-start(), calls=%async_computation.3 | async-start | bytes 13926400 | tf_op jit(solution)/shard_map/reduce_scatter | solution.py:64
  107.2 15.4 %copy-start.3 = (bf16[4,128,2560]{2,1,0:T(8,128)(2,1)S(1)}, bf16[4,128,2560]{2,1,0:T(8,128)(2,1)}, u32[]{:S(2)}) copy-start(bf16[4,128,2560]{2,1,0:T(8,128)(2,1)} %maximum_convert_fusion) | copy-start | bytes 7864324
  121.1 60.3 %collective-permute-start = (bf16[4,128,2560]{2,1,0:T(8,128)(2,1)}, bf16[4,128,2560]{2,1,0:T(8,128)(2,1)S(1)}, u32[]{:S(2)}, u32[]{:S(2)}) collective-permute-start(bf16[4,128,2560]{2,1,0:T(8,128)(2,1)} %bitcast.85), channel_id=1, source_target_pairs={{16,0},{32,16},{48,32},{64,48},{80,64},{96,80},{112,96},{17,1},{33... | collective-permute-start | bytes 7864328 | tf_op jit(solution)/shard_map/ppermute | solution.py:19
  122.6 58.8 %copy-start.4 = (s32[1,128,2560]{2,1,0:T(8,128)S(1)}, s32[1,128,2560]{2,1,0:T(8,128)}, u32[]{:S(2)}) copy-start(s32[1,128,2560]{2,1,0:T(8,128)} %param.16) | copy-start | bytes 3932164
  218.4 123.1 %copy-start.2 = (f32[1,160,2560]{2,1,0:T(8,128)S(1)}, f32[1,160,2560]{2,1,0:T(8,128)}, u32[]{:S(2)}) copy-start(f32[1,160,2560]{2,1,0:T(8,128)} %param.9) | copy-start | bytes 4915204
  218.5 221.5 %copy-start.5 = (bf16[1,32,2560]{2,1,0:T(8,128)(2,1)S(1)}, bf16[1,32,2560]{2,1,0:T(8,128)(2,1)}, u32[]{:S(2)}) copy-start(bf16[1,32,2560]{2,1,0:T(8,128)(2,1)} %param.17) | copy-start | bytes 491524
  218.5 221.5 %all-gather.5.cloned.1.call-start = ((), (), s32[]{:S(2)}) async-start(), calls=%async_computation.2 | async-start | bytes 13926400 | tf_op jit(solution)/shard_map/all_gather | solution.py:85
  439.9 7.9 %copy-start.1 = (bf16[1,4,128,2560]{3,2,1,0:T(8,128)(2,1)S(1)}, bf16[1,4,128,2560]{3,2,1,0:T(8,128)(2,1)}, u32[]{:S(2)}) copy-start(bf16[1,4,128,2560]{3,2,1,0:T(8,128)(2,1)} %param.12) | copy-start | bytes 7864324
Sparse Core Ops, SparseCore 0:
  11.0 96.1 all-gather.2
  218.6 122.9 reduce-scatter.3
  347.7 92.2 all-gather.4
where the time goes:
time: 455 us; the launch traced here: 454 us
  waiting for transfers between devices  354 us (78%)
  matrix products  50.5 us (11%)
  local copies, waits for them, and re-layouts  17.7 us (4%)
  other arithmetic  16.5 us (4%)
  between operations  13.8 us (3%)
    reduce_scatter x1, waiting for transfers between devices, shards(): lax.psum_scatter((partial_value + lax.dot_general(acts_arriving, membrane...  123 us
    all_gather x1, waiting for transfers between devices, shards(): lax.all_gather(fresh_weights, 'dp', axis=0, tiled=True)  92.4 us
    all_gather x1, waiting for transfers between devices, shards(): lax.all_gather(params.astype(jnp.bfloat16), 'dp', axis=0, tiled=True)  92.3 us
    ppermute x1, waiting for transfers between devices, passed_along(): return lax.ppermute(shard, axis, pairs)  46.4 us
    unnamed x13, local copies, waits for them, and re-layouts  17.7 us
    dot_general x1, matrix products, shards(): lax.dot_general(acts_arriving, membrane_arriving, contract, preferred_ele...  16.4 us
    dot_general x1, matrix products, shards(): lax.dot_general(membrane_own, lax.all_gather(params.astype(jnp.bfloat16),...  13.9 us
    dot_general x1, matrix products, shards(): lax.dot_general(acts_own, membrane_own, contract, preferred_element_type=...  12.3 us
  transfers between devices with their start and end apart: 4, of which 4 were waited for; matrix products, arithmetic and copies ran while one was open for 4% of the time, Pallas kernels for 0%

commit v1 on v0

--- a/solution.py
+++ b/solution.py
@@ -46,7 +46,12 @@
     membrane_own = membrane_grads(grads_own[0], windows_own[0]).reshape(flat_rows, features)
     through = lax.dot_general(
         membrane_own,
-        lax.all_gather(params.astype(jnp.bfloat16), "dp", axis=0, tiled=True),
+        jnp.concatenate(
+            lax.all_to_all(
+                jnp.stack([params.astype(jnp.bfloat16)] * lax.axis_size("dp")), "dp", 0, 0
+            ),
+            axis=0,
+        ),
         (((1,), (1,)), ((), ())),
         preferred_element_type=jnp.float32,
     )

time: 455 us -> 526 us (1.16)
  waiting for transfers between devices: 354 us -> 387 us
  local copies, waits for them, and re-layouts: 17.7 us -> 44.5 us
  starting transfers between devices: 1.58 us -> 10.2 us
    all_to_all x0 -> x1, waiting for transfers between devices: none -> 141 us  [shards(): lax.all_to_all(jnp.stack([params.astype(jnp.bfloat16)] * lax.axis_size('d...]
    reduce_scatter x1 -> x0, waiting for transfers between devices: 123 us -> none  [shards(): lax.psum_scatter((partial_value + lax.dot_general(acts_arriving, membrane...]
    unnamed x3, waiting for transfers between devices: 0.05 us -> 116 us
    all_gather x1 -> x0, waiting for transfers between devices: 92.3 us -> none  [shards(): lax.all_gather(params.astype(jnp.bfloat16), 'dp', axis=0, tiled=True)]
    unnamed x13 -> x22, local copies, waits for them, and re-layouts: 17.7 us -> 36.2 us
    all_to_all x0 -> x1, starting transfers between devices: none -> 8.44 us  [shards(): lax.all_to_all(jnp.stack([params.astype(jnp.bfloat16)] * lax.axis_size('d...]
    all_gather x1, waiting for transfers between devices: 92.4 us -> 84.6 us  [shards(): lax.all_gather(fresh_weights, 'dp', axis=0, tiled=True)]
    another operation x0 -> x1, local copies, waits for them, and re-layouts: none -> 6.01 us  [shards(): jnp.stack([params.astype(jnp.bfloat16)] * lax.axis_size('dp'))]
  transfers between devices with their start and end apart: 4 -> 4, of which waited for: 4 -> 4; matrix products, arithmetic and copies ran while one was open for 4% -> 6% of each run, Pallas kernels for 0% -> 0%
where the time goes in v1:
time: 526 us; the launch traced here: 525 us
  waiting for transfers between devices  387 us (74%)
  matrix products  50.5 us (10%)
  local copies, waits for them, and re-layouts  44.5 us (8%)
  other arithmetic  18.3 us (3%)
  between operations  14.1 us (3%)
  starting transfers between devices  10.2 us (2%)
    all_to_all x1, waiting for transfers between devices, shards(): lax.all_to_all(jnp.stack([params.astype(jnp.bfloat16)] * lax.axis_size('d...  141 us
    unnamed x3, waiting for transfers between devices  116 us
    all_gather x1, waiting for transfers between devices, shards(): lax.all_gather(fresh_weights, 'dp', axis=0, tiled=True)  84.6 us
    ppermute x1, waiting for transfers between devices, passed_along(): return lax.ppermute(shard, axis, pairs)  45.7 us
    unnamed x22, local copies, waits for them, and re-layouts  36.2 us
    dot_general x1, matrix products, shards(): lax.dot_general(acts_arriving, membrane_arriving, contract, preferred_ele...  16.4 us
    dot_general x1, matrix products, shards(): lax.dot_general(membrane_own, jnp.concatenate(lax.all_to_all(jnp.stack([p...  13.9 us
    dot_general x1, matrix products, shards(): lax.dot_general(acts_own, membrane_own, contract, preferred_element_type=...  12.3 us
  transfers between devices with their start and end apart: 4, of which 4 were waited for; matrix products, arithmetic and copies ran while one was open for 6% of the time, Pallas kernels for 0%

profile of v1, /device:TPU:1, one launch (start us, length us, event | category | flops | bytes accessed | tf_op | source)
XLA Modules:
  0.0 525.0 jit_solution(12614165933850158711)
XLA Ops:
  7.2 0.0 copy-start
  7.2 1.7 convert_bitcast_fusion
  8.9 6.0 %stack.12 = bf16[16,160,2560]{2,1,0:T(8,128)(2,1)} broadcast(bf16[160,2560]{1,0:T(8,128)(2,1)S(1)} %convert_bitcast_fusion), dimensions={1,2} | broadcast | bytes 13926400 | tf_op jit(solution)/shard_map/stack | solution.py:51
  14.9 8.4 %all-to-all-start = ((bf16[16,160,2560]{2,1,0:T(8,128)(2,1)}), bf16[16,160,2560]{2,1,0:T(8,128)(2,1)}, u32[]{:S(2)}, u32[]{:S(2)}) async-start(bf16[16,160,2560]{2,1,0:T(8,128)(2,1)} %stack.12), calls=%async_computation | async-start | bytes 26214400 | tf_op jit(solution)/shard_map/all_to_all | solution.py:50
  23.3 0.0 reduce-scatter.4.cloned.1.call-start
  23.3 3.2 fusion.12
  26.6 1.8 pad_maximum_fusion
  28.4 141.4 %all-to-all-done = bf16[16,160,2560]{2,1,0:T(8,128)(2,1)} async-done(((bf16[16,160,2560]{2,1,0:T(8,128)(2,1)}), bf16[16,160,2560]{2,1,0:T(8,128)(2,1)}, u32[]{:S(2)}, u32[]{:S(2)}) %all-to-all-start) | async-done | bytes 13107232 | tf_op jit(solution)/shard_map/all_to_all | solution.py:50
  169.7 0.0 copy-start.3
  169.7 13.9 %fusion.1 = bf16[512,2560]{1,0:T(8,128)(2,1)} fusion(bf16[512,2560]{1,0:T(8,128)(2,1)} %bitcast.85, bf16[512,2560]{1,0:T(8,128)(2,1)} %bitcast.86, bf16[2560,2560]{1,0:T(8,128)(2,1)} %bitcast.10), kind=kOutput, calls=%fused_computation.3 | convolution fusion | flops 6714818560 | bytes 20971520 | tf_op jit(solution)/shard_map/dot_general | solution.py:47
  183.6 1.5 collective-permute-start
  185.1 0.0 copy-done
  185.1 0.0 copy-done.3
  185.1 0.0 copy-start.5
  185.1 12.3 %fusion.21 = f32[2560,2560]{1,0:T(8,128)} fusion(bf16[512,2560]{1,0:T(8,128)(2,1)S(1)} %bitcast.87, bf16[512,2560]{1,0:T(8,128)(2,1)S(1)} %bitcast.83), kind=kOutput, calls=%fused_computation.39 | convolution fusion | flops 6710886400 | bytes 31457280 | tf_op jit(solution)/shard_map/dot_general | solution.py:66
  197.4 45.7 %collective-permute-done = bf16[4,128,2560]{2,1,0:T(8,128)(2,1)S(1)} collective-permute-done((bf16[4,128,2560]{2,1,0:T(8,128)(2,1)}, bf16[4,128,2560]{2,1,0:T(8,128)(2,1)S(1)}, u32[]{:S(2)}, u32[]{:S(2)}) %collective-permute-start) | collective-permute-done | bytes 2621472 | tf_op jit(solution)/shard_map/ppermute | solution.py:19
  243.1 0.0 copy-done.5
  243.1 1.2 add_convert_fusion.1
  244.3 1.8 pad_maximum_fusion.1
  246.1 16.4 %fusion = bf16[2560,2560]{0,1:T(8,128)(2,1)} fusion(f32[2560,2560]{1,0:T(8,128)} %fusion.21, bf16[512,2560]{1,0:T(8,128)(2,1)} %bitcast.88, bf16[512,2560]{1,0:T(8,128)(2,1)} %bitcast.89), kind=kOutput, calls=%fused_computation.1 | convolution fusion | flops 6723993600 | bytes 44564480 | tf_op jit(solution)/shard_map/dot_general | solution.py:72
  262.5 17.7 %copy.26 = bf16[2560,2560]{1,0:T(8,128)(2,1)} copy(bf16[2560,2560]{0,1:T(8,128)(2,1)} %fusion) | data formatting | bytes 26214400
  280.2 0.0 copy-start.2
  280.2 0.0 reduce-scatter.4.cloned.1.call-update
  280.2 0.3 all-gather.2.cloned.1.call-start
  280.5 1.1 copy-done.2
  281.6 2.0 copy.19
  283.6 0.0 copy-start.4
  283.6 3.2 copy.20
  286.8 0.0 copy-done.4
  286.8 2.0 copy.21
  288.8 115.7 %reduce-scatter.4.cloned.1.call-done = bf16[160,2560]{1,0:T(8,128)(2,1)} async-done(((bf16[2560,2560]{1,0:T(8,128)(2,1)}), bf16[160,2560]{1,0:T(8,128)(2,1)}) %reduce-scatter.4.cloned.1.call-update) | async-done | bytes 819216
  404.6 2.3 copy.27
  406.9 8.6 %fusion.20 = (bf16[160,2560]{0,1:T(8,128)(2,1)}, f32[160,2560]{0,1:T(8,128)}, f32[1,160,2560]{1,2,0:T(8,128)S(1)}, f32[1,160,2560]{1,2,0:T(8,128)}) fusion(f32[1,160,2560]{1,2,0:T(8,128)} %copy.21, bf16[160,2560]{0,1:T(8,128)(2,1)} %copy.27, f32[1,160,2560]{1,2,0:T(8,128)} %copy.20, f32[1,160,2560]{1,2,0:T(8,128)} %copy.19), kind=kLoop, calls=%fused_computation.38 | loop fusion | flops 6963200 | bytes 11468800 | tf_op jit(solution)/shard_map/convert_element_type | solution.py:86
  415.5 2.3 copy.22
  417.8 0.0 all-gather.2.cloned.1.call-update
  417.8 3.0 copy.23
  420.8 3.0 copy.24
  423.8 0.0 copy-start.6
  423.8 1.8 copy.25
  425.6 84.6 %all-gather.2.cloned.1.call-done = bf16[2560,2560]{1,0:T(8,128)(2,1)} async-done(((bf16[160,2560]{1,0:T(8,128)(2,1)}), bf16[2560,2560]{1,0:T(8,128)(2,1)}) %all-gather.2.cloned.1.call-update) | async-done | bytes 13107216 | tf_op jit(solution)/shard_map/all_gather | solution.py:90
  510.3 0.0 copy-done.6
  510.3 0.0 copy-start.1
  510.3 7.9 %fusion.2 = bf16[1,32,2560]{2,1,0:T(8,128)(2,1)} fusion(bf16[2560,2560]{1,0:T(8,128)(2,1)} %all-gather.2.cloned.1.call-done, bf16[1,32,2560]{2,1,0:T(8,128)(2,1)S(1)} %copy-done.6), kind=kOutput, calls=%fused_computation.6 | convolution fusion | flops 419512320 | bytes 13434880 | tf_op jit(solution)/shard_map/dot_general | solution.py:88
  518.1 0.0 copy-done.1
Async XLA Ops:
  7.2 177.9 %copy-start = (bf16[1,4,128,2560]{3,2,1,0:T(8,128)(2,1)S(1)}, bf16[1,4,128,2560]{3,2,1,0:T(8,128)(2,1)}, u32[]{:S(2)}) copy-start(bf16[1,4,128,2560]{3,2,1,0:T(8,128)(2,1)} %param.12) | copy-start | bytes 7864324
  14.9 154.9 %all-to-all-start = ((bf16[16,160,2560]{2,1,0:T(8,128)(2,1)}), bf16[16,160,2560]{2,1,0:T(8,128)(2,1)}, u32[]{:S(2)}, u32[]{:S(2)}) async-start(bf16[16,160,2560]{2,1,0:T(8,128)(2,1)} %stack.12), calls=%async_computation | async-start | bytes 26214400 | tf_op jit(solution)/shard_map/all_to_all | solution.py:50
  23.3 381.3 %reduce-scatter.4.cloned.1.call-start = ((), (), s32[]{:S(2)}) async-start(), calls=%async_computation.3 | async-start | bytes 13926400
  169.7 15.4 %copy-start.3 = (bf16[4,128,2560]{2,1,0:T(8,128)(2,1)S(1)}, bf16[4,128,2560]{2,1,0:T(8,128)(2,1)}, u32[]{:S(2)}) copy-start(bf16[4,128,2560]{2,1,0:T(8,128)(2,1)} %pad_maximum_fusion) | copy-start | bytes 7864324
  183.6 59.5 %collective-permute-start = (bf16[4,128,2560]{2,1,0:T(8,128)(2,1)}, bf16[4,128,2560]{2,1,0:T(8,128)(2,1)S(1)}, u32[]{:S(2)}, u32[]{:S(2)}) collective-permute-start(bf16[4,128,2560]{2,1,0:T(8,128)(2,1)} %bitcast.90), channel_id=1, source_target_pairs={{16,0},{32,16},{48,32},{64,48},{80,64},{96,80},{112,96},{17,1},{33... | collective-permute-start | bytes 7864328 | tf_op jit(solution)/shard_map/ppermute | solution.py:19
  185.1 58.0 %copy-start.5 = (s32[1,128,2560]{2,1,0:T(8,128)S(1)}, s32[1,128,2560]{2,1,0:T(8,128)}, u32[]{:S(2)}) copy-start(s32[1,128,2560]{2,1,0:T(8,128)} %param.16) | copy-start | bytes 3932164
  280.2 1.4 copy-start.2
  280.2 230.1 %all-gather.2.cloned.1.call-start = ((), (), s32[]{:S(2)}) async-start(), calls=%async_computation.2 | async-start | bytes 13926400 | tf_op jit(solution)/shard_map/all_gather | solution.py:90
  283.6 3.2 copy-start.4
  423.8 86.4 %copy-start.6 = (bf16[1,32,2560]{2,1,0:T(8,128)(2,1)S(1)}, bf16[1,32,2560]{2,1,0:T(8,128)(2,1)}, u32[]{:S(2)}) copy-start(bf16[1,32,2560]{2,1,0:T(8,128)(2,1)} %param.17) | copy-start | bytes 491524
  510.3 7.9 %copy-start.1 = (bf16[1,4,128,2560]{3,2,1,0:T(8,128)(2,1)S(1)}, bf16[1,4,128,2560]{3,2,1,0:T(8,128)(2,1)}, u32[]{:S(2)}) copy-start(bf16[1,4,128,2560]{3,2,1,0:T(8,128)(2,1)} %param.12) | copy-start | bytes 7864324
Sparse Core Ops, SparseCore 0:
  280.3 124.2 reduce-scatter.3
  418.0 92.2 all-gather.1
